TPU v7x, 128 devices: a whole 4x4x4 slice. The times are simulated.
128 devices in a mesh: dp: 4 (over y_hi, core), ctx: 32 (over x, y_lo, z).
Axes of the slice: x: 4, y: 4 (y_hi: 2, y_lo: 2; y = y_hi * 2 + y_lo), z: 4, core: 2. Of those that a mesh axis runs over, the one named last changes fastest.
Arguments:
- queries: bfloat16 [16384, 2048], P(('dp', 'ctx')), parts along dimension 0, may hold values from -9 to 9
- keys: bfloat16 [16384, 512], P(('dp', 'ctx')), parts along dimension 0, may hold values from -9 to 9
- values: bfloat16 [16384, 512], P(('dp', 'ctx')), parts along dimension 0, may hold values from -6 to 6
- grad_out: bfloat16 [16384, 2048], P(('dp', 'ctx')), parts along dimension 0, may hold values from -6 to 6
- positions: int32 [1024], P('dp'), parts along dimension 0, may hold values from 0 to 4095, as said below
Outputs:
- attended: bfloat16 [16384, 2048], P(('dp', 'ctx')), parts along dimension 0
- grad_queries: bfloat16 [16384, 2048], P(('dp', 'ctx')), parts along dimension 0
- grad_keys: bfloat16 [16384, 512], P(('dp', 'ctx')), parts along dimension 0
- grad_values: bfloat16 [16384, 512], P(('dp', 'ctx')), parts along dimension 0
There are 4 independent parts, one for each index of `dp`. A program takes and returns all parts, laid end to end along the dimension named above; each array names one. Nothing has to cross between parts.
Inputs may be any that keep to these rules, and one draw needn't show every extreme that they name: 256 distinct token positions in increasing order; the 128 tokens of one index of ctx hold at most 32 of them, and one index holds exactly 32.
All inputs are finite; a program needn't handle non-finite values.
Results may differ from a plain program's by a relative error of at most 0.0075.
Values may be sent and summed in bfloat16 or wider, within the bound.
No kernel may reach another device: no remote copies, remote signals or barrier semaphores. Data moves between devices by JAX's collectives and lax.ppermute only.
A program may use at most 192 MiB of HBM per device.

v0:
```python
import math

import jax
import jax.numpy as jnp
from jax import lax
from jax.sharding import PartitionSpec as P

HQ = 16
HK = 4
DH = 128
BLOCK = 64
CAP = 32


highest = lax.Precision.HIGHEST


def with_halo(array, sides, width):
    for axis, dim in sides:
        size, length = (lax.axis_size(axis), array.shape[dim])
        up = [(i, (i + 1) % size) for i in range(size - 1)]
        down = [(j, i) for i, j in up]
        last = lax.slice_in_dim(array, length - width, length, axis=dim)
        first = lax.slice_in_dim(array, 0, width, axis=dim)
        before = lax.ppermute(last, axis, up)
        after = lax.ppermute(first, axis, down)
        array = jnp.concatenate([before, array, after], axis=dim)
    return array


def combined_all(part, axis, combine):
    gathered = jax.tree.map(lambda a: lax.all_gather(a, axis), part)

    def take(source):
        return jax.tree.map(lambda a: lax.dynamic_index_in_dim(a, source, 0, False), gathered)

    return lax.fori_loop(
        1, lax.axis_size(axis), lambda source, state: combine(state, take(source)), take(0)
    )


def window_group(pieces, glob_keys, glob_values, score_scale):
    query_block, grad_block, key_window, value_window, key_usable, query_live = pieces
    near = (
        jnp.einsum("bqard,bkad->barqk", query_block, key_window, preferred_element_type=jnp.float32)
        * score_scale
    )
    far = (
        jnp.einsum("bqard,gad->barqg", query_block, glob_keys, preferred_element_type=jnp.float32)
        * score_scale
    )
    near = jnp.where(key_usable[:, None, None, None, :], near, -jnp.inf)
    row_top = jnp.maximum(jnp.max(near, axis=-1), jnp.max(far, axis=-1))
    near_weight = jnp.exp(near - row_top[..., None])
    far_weight = jnp.exp(far - row_top[..., None])
    total = jnp.sum(near_weight, axis=-1) + jnp.sum(far_weight, axis=-1)
    mixed = jnp.einsum(
        "barqk,bkad->bqard",
        near_weight.astype(jnp.bfloat16),
        value_window,
        preferred_element_type=jnp.float32,
    )
    mixed = mixed + jnp.einsum(
        "barqg,gad->bqard",
        far_weight.astype(jnp.bfloat16),
        glob_values,
        preferred_element_type=jnp.float32,
    )
    attended = mixed / jnp.transpose(total, (0, 3, 1, 2))[..., None]
    delta = jnp.transpose(jnp.sum(grad_block * attended, axis=-1), (0, 2, 3, 1))
    live = query_live[:, None, None, :, None]
    near_prob = near_weight / total[..., None]
    far_prob = far_weight / total[..., None]
    near_dprob = jnp.einsum(
        "bqard,bkad->barqk", grad_block, value_window, preferred_element_type=jnp.float32
    )
    far_dprob = jnp.einsum(
        "bqard,gad->barqg", grad_block, glob_values, preferred_element_type=jnp.float32
    )
    near_dscore = (near_prob * (near_dprob - delta[..., None]) * live).astype(jnp.bfloat16)
    far_dscore = (far_prob * (far_dprob - delta[..., None]) * live).astype(jnp.bfloat16)
    near_round = (near_prob * live).astype(jnp.bfloat16)
    far_round = (far_prob * live).astype(jnp.bfloat16)
    grad_query = jnp.einsum(
        "barqk,bkad->bqard", near_dscore, key_window, preferred_element_type=jnp.float32
    )
    grad_query = score_scale * (
        grad_query
        + jnp.einsum("barqg,gad->bqard", far_dscore, glob_keys, preferred_element_type=jnp.float32)
    )
    grad_key_win = score_scale * jnp.einsum(
        "barqk,bqard->bkad", near_dscore, query_block, preferred_element_type=jnp.float32
    )
    grad_value_win = jnp.einsum(
        "barqk,bqard->bkad", near_round, grad_block, preferred_element_type=jnp.float32
    )
    grad_key_glob = score_scale * jnp.einsum(
        "barqg,bqard->gad", far_dscore, query_block, preferred_element_type=jnp.float32
    )
    grad_value_glob = jnp.einsum(
        "barqg,bqard->gad", far_round, grad_block, preferred_element_type=jnp.float32
    )
    return (attended, grad_query, grad_key_win, grad_value_win, grad_key_glob, grad_value_glob)


def combine_softmax(left_part, right_part):
    left_top, left_total, left_summed = left_part
    right_top, right_total, right_summed = right_part
    joint_top = jnp.maximum(left_top, right_top)
    left_factor = jnp.exp(left_top - joint_top)
    right_factor = jnp.exp(right_top - joint_top)
    return (
        joint_top,
        left_total * left_factor + right_total * right_factor,
        left_summed * left_factor[..., None] + right_summed * right_factor[..., None],
    )


def local(queries, keys, values, grad_out, positions):
    tok_rows = queries.shape[0]
    query_width = queries.shape[1]
    key_width = keys.shape[1]
    q_per_kv = HQ // HK
    ctx_count = lax.axis_size("ctx")
    seq_total = tok_rows * ctx_count
    first_row = lax.axis_index("ctx") * tok_rows
    score_scale = 1.0 / math.sqrt(DH)
    glob_count = positions.shape[0]
    local_row = positions - first_row
    is_mine = (local_row >= 0) & (local_row < tok_rows)
    safe_row = jnp.clip(local_row, 0, tok_rows - 1)
    before = jnp.sum((positions < first_row).astype(jnp.int32))
    held_count = jnp.sum(is_mine.astype(jnp.int32))
    slot_index = jnp.arange(CAP)
    slot_ok = slot_index < held_count
    slot_row = jnp.clip(
        positions[jnp.clip(before + slot_index, 0, glob_count - 1)] - first_row, 0, tok_rows - 1
    )
    owner_index = positions // tok_rows
    owner_start = jnp.sum((owner_index[None, :] < owner_index[:, None]).astype(jnp.int32), axis=1)
    slot_of = owner_index * CAP + jnp.arange(glob_count) - owner_start
    packed = jnp.concatenate(
        [queries[slot_row], keys[slot_row], values[slot_row], grad_out[slot_row]], axis=1
    )
    packed = jnp.where(slot_ok[:, None], packed, jnp.zeros_like(packed))
    everyone = lax.all_gather(packed, "ctx", axis=0, tiled=True)
    compact = everyone[slot_of]
    glob_query = compact[:, :query_width].reshape(glob_count, HK, q_per_kv, DH)
    glob_keys = compact[:, query_width : query_width + key_width].reshape(glob_count, HK, DH)
    glob_values = compact[:, query_width + key_width : query_width + 2 * key_width].reshape(
        glob_count, HK, DH
    )
    glob_grad = compact[:, query_width + 2 * key_width :].reshape(glob_count, HK, q_per_kv, DH)
    paired = jnp.concatenate([keys, values], axis=1)
    extended = with_halo(paired, (("ctx", 0),), BLOCK)
    blocks = tok_rows // BLOCK
    ext_blocks = extended.reshape(blocks + 2, BLOCK, 2 * key_width)
    window = jnp.concatenate([ext_blocks[:-2], ext_blocks[1:-1], ext_blocks[2:]], axis=1)
    key_window = window[:, :, :key_width].reshape(blocks, 3 * BLOCK, HK, DH)
    value_window = window[:, :, key_width:].reshape(blocks, 3 * BLOCK, HK, DH)
    ext_position = first_row - BLOCK + jnp.arange(tok_rows + 2 * BLOCK)
    ext_global = jnp.any(ext_position[:, None] == positions[None, :], axis=1)
    ext_usable = (
        (ext_position >= 0) & (ext_position < seq_total) & jnp.logical_not(ext_global)
    ).reshape(blocks + 2, BLOCK)
    key_usable = jnp.concatenate([ext_usable[:-2], ext_usable[1:-1], ext_usable[2:]], axis=1)
    query_live = (
        jnp.logical_not(ext_global[BLOCK : BLOCK + tok_rows])
        .astype(jnp.float32)
        .reshape(blocks, BLOCK)
    )
    per_step = min(8, blocks)
    step_count = blocks // per_step

    def regroup(source):
        return source.reshape((step_count, per_step) + source.shape[1:])

    stacked = (
        regroup(queries.reshape(blocks, BLOCK, HK, q_per_kv, DH)),
        regroup(grad_out.reshape(blocks, BLOCK, HK, q_per_kv, DH)),
        regroup(key_window),
        regroup(value_window),
        regroup(key_usable),
        regroup(query_live),
    )
    results = lax.map(
        lambda pieces: window_group(pieces, glob_keys, glob_values, score_scale), stacked
    )
    attended_loc = results[0].reshape(tok_rows, query_width)
    grad_query_loc = results[1].reshape(tok_rows, query_width)
    window_grads = jnp.concatenate(
        [
            results[2].reshape(blocks, 3, BLOCK, key_width),
            results[3].reshape(blocks, 3, BLOCK, key_width),
        ],
        axis=3,
    )
    glob_key_grad = jnp.sum(results[4], axis=0).reshape(glob_count, key_width)
    glob_value_grad = jnp.sum(results[5], axis=0).reshape(glob_count, key_width)
    key_here = keys.reshape(tok_rows, HK, DH)
    value_here = values.reshape(tok_rows, HK, DH)
    glob_score = (
        jnp.einsum("gard,uad->argu", glob_query, key_here, preferred_element_type=jnp.float32)
        * score_scale
    )
    top_here = jnp.max(glob_score, axis=-1)
    weight_here = jnp.exp(glob_score - top_here[..., None])
    total_here = jnp.sum(weight_here, axis=-1)
    summed_here = jnp.einsum(
        "argu,uad->argd", weight_here, value_here.astype(jnp.float32), precision=highest
    )
    glob_top, glob_total, glob_summed = combined_all(
        (top_here, total_here, summed_here), "ctx", combine_softmax
    )
    glob_attended = glob_summed / glob_total[..., None]
    glob_delta = jnp.sum(
        jnp.transpose(glob_grad, (1, 2, 0, 3)).astype(jnp.float32) * glob_attended, axis=-1
    )
    glob_prob = jnp.exp(glob_score - glob_top[..., None]) / glob_total[..., None]
    glob_dprob = jnp.einsum(
        "gard,uad->argu", glob_grad, value_here, preferred_element_type=jnp.float32
    )
    glob_dscore = (glob_prob * (glob_dprob - glob_delta[..., None])).astype(jnp.bfloat16)
    glob_round = glob_prob.astype(jnp.bfloat16)
    glob_query_grad = score_scale * jnp.einsum(
        "argu,uad->gard", glob_dscore, key_here, preferred_element_type=jnp.float32
    )
    key_grad_here = score_scale * jnp.einsum(
        "argu,gard->uad", glob_dscore, glob_query, preferred_element_type=jnp.float32
    )
    value_grad_here = jnp.einsum(
        "argu,gard->uad", glob_round, glob_grad, preferred_element_type=jnp.float32
    )
    empty_block = jnp.zeros((1, BLOCK, 2 * key_width), jnp.float32)
    spread = jnp.concatenate([window_grads[:, 0], empty_block, empty_block], axis=0)
    spread = spread + jnp.concatenate([empty_block, window_grads[:, 1], empty_block], axis=0)
    spread = spread + jnp.concatenate([empty_block, empty_block, window_grads[:, 2]], axis=0)
    rims = jnp.concatenate([spread[0], spread[-1]], axis=0)
    arrived = with_halo(rims, (("ctx", 0),), BLOCK)
    pair_grad = spread[1:-1].reshape(tok_rows, 2 * key_width)
    pair_grad = pair_grad.at[:BLOCK].add(arrived[:BLOCK])
    pair_grad = pair_grad.at[tok_rows - BLOCK :].add(arrived[3 * BLOCK :])
    pair_grad = pair_grad + jnp.concatenate(
        [key_grad_here.reshape(tok_rows, key_width), value_grad_here.reshape(tok_rows, key_width)],
        axis=1,
    )
    glob_grads = jnp.concatenate(
        [glob_query_grad.reshape(glob_count, query_width), glob_key_grad, glob_value_grad], axis=1
    )
    laid = (
        jnp.zeros((ctx_count * CAP, glob_grads.shape[1]), jnp.float32).at[slot_of].set(glob_grads)
    )
    returned = lax.psum_scatter(laid, "ctx", scatter_dimension=0, tiled=True)
    target = jnp.where(slot_ok, slot_row, tok_rows)
    grad_query_all = grad_query_loc.at[target].add(returned[:, :query_width], mode="drop")
    pair_grad = pair_grad.at[target].add(returned[:, query_width:], mode="drop")
    glob_rows_out = jnp.transpose(glob_attended, (2, 0, 1, 3)).reshape(glob_count, query_width)
    attended_all = attended_loc.at[jnp.where(is_mine, safe_row, tok_rows)].set(
        glob_rows_out, mode="drop"
    )
    return (
        attended_all.astype(jnp.bfloat16),
        grad_query_all.astype(jnp.bfloat16),
        pair_grad[:, :key_width].astype(jnp.bfloat16),
        pair_grad[:, key_width:].astype(jnp.bfloat16),
    )


def solution(mesh):
    in_specs = (
        P(("dp", "ctx"), None),
        P(("dp", "ctx"), None),
        P(("dp", "ctx"), None),
        P(("dp", "ctx"), None),
        P("dp"),
    )
    out_specs = (
        P(("dp", "ctx"), None),
        P(("dp", "ctx"), None),
        P(("dp", "ctx"), None),
        P(("dp", "ctx"), None),
    )
    return jax.shard_map(local, mesh=mesh, in_specs=in_specs, out_specs=out_specs, check_vma=False)
```

profile of v0, /device:TPU:0, one launch (start us, length us, event | category | flops | bytes accessed | tf_op | source)
XLA Modules:
  0.0 1261.8 jit_solution(1637269885959705187)
XLA Ops:
  18.9 171.2 %all-gather.6.cloned.1.call-done = bf16[1024,5120]{1,0:T(8,128)(2,1)} async-done(((bf16[32,5120]{1,0:T(8,128)(2,1)}), bf16[1024,5120]{1,0:T(8,128)(2,1)}) %all-gather.6.cloned.1.call-update) | async-done | bytes 10485776 | tf_op jit(solution)/shard_map/all_gather | solution.py:146
  190.0 10.0 gather_fusion.5
  204.8 3.2 fusion.24
  218.5 3.4 collective-permute-done.1
  228.8 89.1 %all-gather.1 = f32[128,4,256]{2,1,0:T(4,128)S(1)} all-gather(f32[4,4,256]{2,1,0:T(4,128)S(1)} %fusion.26), channel_id=3, replica_groups=mesh['dp'=4,'ctx'=32] {'ctx'}, dimensions={0}, use_global_device_ids=true | all-gather | bytes 540672 | tf_op jit(solution)/shard_map/all_gather | solution.py:32
  317.8 85.6 %all-gather = f32[128,4,256]{2,1,0:T(4,128)S(1)} all-gather(f32[4,4,256]{2,1,0:T(4,128)S(1)} %copy-done.36), channel_id=2, replica_groups=mesh['dp'=4,'ctx'=32] {'ctx'}, dimensions={0}, use_global_device_ids=true | all-gather | bytes 540672 | tf_op jit(solution)/shard_map/all_gather | solution.py:32
  423.7 507.2 %all-gather.8.cloned.1.call-done = f32[128,4,256,128]{3,2,1,0:T(8,128)} async-done(((f32[4,4,256,128]{3,2,1,0:T(8,128)}), f32[128,4,256,128]{3,2,1,0:T(8,128)}) %all-gather.8.cloned.1.call-update) | async-done | bytes 67108880 | tf_op jit(solution)/shard_map/all_gather | solution.py:32
  932.7 108.1 %while.14 = (s32[]{:T(128)}, f32[4,4,256]{2,1,0:T(4,128)S(1)}, f32[4,4,256]{2,1,0:T(4,128)S(1)}, f32[4,4,256,128]{3,2,1,0:T(8,128)S(1)}, f32[32,4,4,256]{3,2,1,0...) while((s32[]{:T(128)}, f32[4,4,256]{2,1,0:T(4,128)S(1)}, ...), condition=%wide.region_11.12_spmd, body=%wide.region_10.11_spmd.sunk | while | flops 1597445 | bytes 6455447 | solution.py:37
  933.4 2.7 fusion.128
  936.9 2.7 fusion.128
  940.4 2.7 fusion.128
  943.9 2.7 fusion.128
  947.4 2.7 fusion.128
  950.9 2.7 fusion.128
  954.4 2.7 fusion.128
  957.8 2.7 fusion.128
  1024.1 2.7 fusion.128
  1042.6 3.7 fusion.10
  1049.9 2.9 copy.237
  1052.8 9.4 scatter_custom_fusion.1
  1062.3 2.8 fusion.18
  1068.9 3.0 convolution_bitcast_fusion.4
  1085.4 2.9 copy.208
  1110.3 140.1 %reduce-scatter.2.cloned.1.call-done = f32[32,3072]{1,0:T(8,128)} async-done(((f32[1024,3072]{1,0:T(8,128)}), f32[32,3072]{1,0:T(8,128)}) %reduce-scatter.2.cloned.1.call-update) | async-done | bytes 393232 | tf_op jit(solution)/shard_map/reduce_scatter | solution.py:253
  (257 shorter events, 187.5 us)
Async XLA Ops:
  7.2 7.8 copy-start.8
  7.2 8.5 copy-start.17
  7.2 9.1 copy-start.18
  7.2 182.8 %all-gather.6.cloned.1.call-start = ((), (), s32[]{:S(2)}) async-start(), calls=%async_computation.1 | async-start | bytes 10813440 | tf_op jit(solution)/shard_map/all_gather | solution.py:146
  17.8 913.1 %all-gather.8.cloned.1.call-start = ((), (), s32[]{:S(2)}) async-start(), calls=%async_computation.3 | async-start | bytes 69206016 | tf_op jit(solution)/shard_map/all_gather | solution.py:32
  17.9 186.3 %copy-start.29 = (bf16[128,4,128]{2,1,0:T(4,128)(2,1)}, bf16[128,4,128]{2,1,0:T(4,128)(2,1)S(1)}, u32[]{:S(2)}) copy-start(bf16[128,4,128]{2,1,0:T(4,128)(2,1)S(1)} %reshape.264) | copy-start | bytes 393220
  18.1 185.6 %copy-start.20 = (bf16[128,4,128,1]{0,2,3,1:T(8,128)(2,1)}, bf16[128,4,128,1]{0,2,3,1:T(8,128)(2,1)S(1)}, u32[]{:S(2)}) copy-start(bf16[128,4,128,1]{0,2,3,1:T(8,128)(2,1)S(1)} %copy.266) | copy-start | bytes 393220
  204.2 24.2 %copy-start.1 = (f32[4,256,4,128]{1,3,2,0:T(8,128)}, f32[4,256,4,128]{1,3,2,0:T(8,128)S(1)}, u32[]{:S(2)}) copy-start(f32[4,256,4,128]{1,3,2,0:T(8,128)S(1)} %get-tuple-element.307) | copy-start | bytes 6291460
  208.1 6.0 copy-start
  208.1 7.5 copy-start.7
  208.1 8.6 copy-start.9
  208.1 1042.4 %reduce-scatter.2.cloned.1.call-start = ((), (), s32[]{:S(2)}) async-start(), calls=%async_computation.2 | async-start | bytes 12976128 | tf_op jit(solution)/shard_map/reduce_scatter | solution.py:253
  209.8 8.7 collective-permute-start
  212.3 9.6 collective-permute-start.1
  218.5 7.4 copy-start.40
  228.4 89.5 %copy-start.36 = (f32[4,4,256]{2,1,0:T(4,128)S(1)}, f32[4,4,256]{2,1,0:T(4,128)}, u32[]{:S(2)}) copy-start(f32[4,4,256]{2,1,0:T(4,128)} %copy-done.34) | copy-start | bytes 49156
  317.8 87.0 %copy-start.24 = (f32[128,4,256]{2,1,0:T(4,128)}, f32[128,4,256]{2,1,0:T(4,128)S(1)}, u32[]{:S(2)}) copy-start(f32[128,4,256]{2,1,0:T(4,128)S(1)} %all-gather.1) | copy-start | bytes 1572868
  409.7 652.5 %copy-start.32 = (f32[2,4,4,64]{3,2,1,0:T(4,128)}, f32[2,4,4,64]{3,2,1,0:T(4,128)S(1)}, u32[]{:S(2)}) copy-start(f32[2,4,4,64]{3,2,1,0:T(4,128)S(1)} %copy_maximum_fusion) | copy-start | bytes 24580
  411.7 650.5 %copy-start.38 = (f32[2,4,4,64]{3,2,1,0:T(4,128)}, f32[2,4,4,64]{3,2,1,0:T(4,128)S(1)}, u32[]{:S(2)}) copy-start(f32[2,4,4,64]{3,2,1,0:T(4,128)S(1)} %copy_add_fusion) | copy-start | bytes 24580
  423.7 509.0 %copy-start.26 = (f32[4,4,256]{2,1,0:T(4,128)S(1)}, f32[4,4,256]{2,1,0:T(4,128)}, u32[]{:S(2)}) copy-start(f32[4,4,256]{2,1,0:T(4,128)} %slice.194) | copy-start | bytes 49156
  1078.1 13.6 %collective-permute-start.2 = (f32[64,1024]{1,0:T(8,128)}, f32[64,1024]{1,0:T(8,128)}, u32[]{:S(2)}, u32[]{:S(2)}) collective-permute-start(f32[64,1024]{1,0:T(8,128)} %get-tuple-element.286), channel_id=1, source_target_pairs={{0,1},{1,2},{2,3},{3,4},{4,5},{5,6},{6,7},{7,8},{8,9},{9,10},{10,1... | collective-permute-start | bytes 786440 | tf_op jit(solution)/shard_map/ppermute | solution.py:25
  1080.2 15.4 %collective-permute-start.3 = (f32[64,1024]{1,0:T(8,128)}, f32[64,1024]{1,0:T(8,128)}, u32[]{:S(2)}, u32[]{:S(2)}) collective-permute-start(f32[64,1024]{1,0:T(8,128)} %get-tuple-element.285), channel_id=1, source_target_pairs={{1,0},{2,1},{3,2},{4,3},{5,4},{6,5},{7,6},{8,7},{9,8},{10,9},{11,1... | collective-permute-start | bytes 786440 | tf_op jit(solution)/shard_map/ppermute | solution.py:26
  1088.3 9.1 copy-start.28
  1109.1 143.6 %copy-start.13 = (f32[128,2048]{1,0:T(8,128)S(1)}, f32[128,2048]{1,0:T(8,128)}, u32[]{:S(2)}) copy-start(f32[128,2048]{1,0:T(8,128)} %reshape.266) | copy-start | bytes 3145732
  (30 other events, 73.0 us)
Sparse Core Ops, SparseCore 0:
  17.9 172.0 all-gather.5
  208.2 722.6 all-gather.7
  1062.4 188.0 reduce-scatter.1
where the time goes:
time: 1280 us; the launch traced here: 1260 us
  waiting for transfers between devices  826 us (65%)
  blocking collectives  175 us (14%)
  other arithmetic  140 us (11%)
  local copies, waits for them, and re-layouts  70.2 us (5%)
  matrix products  27.7 us (2%)
  between operations  14.7 us (1%)
    all_gather x1, waiting for transfers between devices, combined_all(): gathered = jax.tree.map(lambda a: lax.all_gather(a, axis), part)  507 us
    all_gather x2, blocking collectives, combined_all(): gathered = jax.tree.map(lambda a: lax.all_gather(a, axis), part)  175 us
    all_gather x1, waiting for transfers between devices, local(): everyone = lax.all_gather(packed, 'ctx', axis=0, tiled=True)  171 us
    reduce_scatter x1, waiting for transfers between devices, local(): returned = lax.psum_scatter(laid, 'ctx', scatter_dimension=0, tiled=True)  140 us
    add x31, other arithmetic, combine_softmax(): left_summed * left_factor[..., None]  83.3 us
  transfers between devices with their start and end apart: 7, of which 6 were waited for; matrix products, arithmetic and copies ran while one was open for 6% of the time, Pallas kernels for 0%

commit v1 on v0

v1 whole, which is shorter than its diff:
```python
import functools
import math

import jax
import jax.numpy as jnp
from jax import lax
from jax.experimental import pallas as pl
from jax.experimental.pallas import tpu as pltpu
from jax.sharding import PartitionSpec as P

HQ = 16
HK = 4
DH = 128
BLOCK = 64
REP = HQ // HK
GROUP = 4
CHUNK = 64
TILE = 512
ROWS = REP * BLOCK
SCALE = 1.0 / math.sqrt(DH)
EXP2 = SCALE * math.log2(math.e)
NEG = -1e30

F32 = jnp.float32
BF16 = jnp.bfloat16


def dot_nt(a, b):
    return lax.dot_general(a, b, (((1,), (1,)), ((), ())), preferred_element_type=F32)


def dot_nn(a, b):
    return lax.dot_general(a, b, (((1,), (0,)), ((), ())), preferred_element_type=F32)


def iota(shape, dim):
    return lax.broadcasted_iota(jnp.int32, shape, dim)


def prep_kernel(clusters, q_ref, k_ref, v_ref, g_ref, kv_ref, *qg_refs):
    z = lax.rem(lax.axis_index("ctx"), GROUP)
    wide = REP * DH
    for j in range(HK):
        one = jnp.concatenate(
            [k_ref[:, j * DH : (j + 1) * DH], v_ref[:, j * DH : (j + 1) * DH]], axis=1
        )
        for s in range(clusters):
            kv_ref[s * GROUP + j] = one
    for step in range(GROUP):
        col = pl.multiple_of(lax.rem(z + step, GROUP) * wide, wide)
        qg_refs[step][:, :wide] = q_ref[:, pl.ds(col, wide)]
        qg_refs[step][:, wide:] = g_ref[:, pl.ds(col, wide)]


def main_kernel(
    seq, toks, glob, bounds_ref, pos_ref, kv_hbm, *refs
):
    qg_in = refs[:GROUP]
    dkv_out = refs[GROUP]
    qg_out = refs[GROUP + 1 : 2 * GROUP + 1]
    (kvp, kvt, dkv, dkv_bf, qg, out, sc, dp, attg, kg, kgt, dkg, kv_sem, qg_sem, out_sem, dkv_sem) = refs[
        2 * GROUP + 1 :
    ]
    me = lax.axis_index("ctx")
    z = lax.rem(me, GROUP)
    ctoks = GROUP * toks
    wide = REP * DH
    tiles = seq // TILE
    first = (me // GROUP) * ctoks

    kv_copy = pltpu.make_async_copy(kv_hbm, kvp.at[pl.ds(BLOCK, seq)], kv_sem)
    kv_copy.start()
    qg_copies = []
    for step in range(GROUP):
        src = lax.rem(z + GROUP - step, GROUP)
        copy = pltpu.make_async_copy(
            qg_in[step], qg.at[pl.ds(pl.multiple_of(src * toks, toks), toks)], qg_sem.at[step]
        )
        copy.start()
        qg_copies.append(copy)

    kvp[0:BLOCK] = jnp.zeros((BLOCK, 2 * DH), BF16)
    kvp[BLOCK + seq : 2 * BLOCK + seq] = jnp.zeros((BLOCK, 2 * DH), BF16)
    dkv[...] = jnp.zeros_like(dkv)
    attg[...] = jnp.zeros_like(attg)
    dkg[...] = jnp.zeros_like(dkg)
    pos_row = pos_ref[...]
    eye = iota((glob, glob), 0) == iota((glob, glob), 1)
    pos_col = jnp.sum(
        jnp.where(eye, jnp.broadcast_to(pos_row, (glob, glob)), 0).astype(F32), axis=1, keepdims=True
    ).astype(jnp.int32)
    before = bounds_ref[0]
    count = bounds_ref[1] - before

    for copy in qg_copies:
        copy.wait()
    kv_copy.wait()

    def gather_tile(t, acc):
        off = pl.multiple_of(t * TILE, TILE)
        tile = kvp[pl.ds(pl.multiple_of(off + BLOCK, BLOCK), TILE), :]
        kvt[:, pl.ds(off, TILE)] = tile.T
        hot = (pos_col == off + iota((glob, TILE), 1)).astype(F32).astype(BF16)
        return acc + dot_nn(hot, tile)

    got = lax.fori_loop(0, tiles, gather_tile, jnp.zeros((glob, 2 * DH), F32)).astype(BF16)
    kg[...] = got
    kgt[...] = got.T

    tok_row = first + iota((1, ctoks), 1)
    is_row = jnp.sum((pos_col == tok_row).astype(F32), axis=0, keepdims=True)
    rank_row = jnp.sum((pos_col < tok_row).astype(F32), axis=0, keepdims=True)
    slot_row = jnp.where(is_row > 0.5, rank_row.astype(jnp.int32) - before, -1)

    def chunk(ch, carry):
        base = ch * CHUNK
        hot = (slot_row == base + iota((CHUNK, ctoks), 0)).astype(F32).astype(BF16)
        picked = dot_nn(hot, qg[...]).astype(BF16)
        q = jnp.concatenate([picked[:, h * DH : (h + 1) * DH] for h in range(REP)], axis=0)
        g = jnp.concatenate([picked[:, wide + h * DH : wide + (h + 1) * DH] for h in range(REP)], axis=0)
        valid = (base + lax.rem(iota((1, ROWS), 1), CHUNK) < count).astype(F32)

        def fold(x):
            parts = [x[8 * i : 8 * i + 8] for i in range(TILE // 8)]
            return parts

        def pass_a(t, top):
            off = pl.multiple_of(t * TILE, TILE)
            k = kvp[pl.ds(pl.multiple_of(off + BLOCK, BLOCK), TILE), :DH]
            s = dot_nt(k, q)
            sc[pl.ds(off, TILE), :] = s
            return jnp.maximum(top, jnp.max(s, axis=0, keepdims=True))

        top = lax.fori_loop(0, tiles, pass_a, jnp.full((1, ROWS), NEG, F32))

        def pass_b(t, state):
            total, dsum, mixed = state
            off = pl.multiple_of(t * TILE, TILE)
            v = kvp[pl.ds(pl.multiple_of(off + BLOCK, BLOCK), TILE), DH:]
            w = jnp.exp2((sc[pl.ds(off, TILE), :] - top) * EXP2)
            d = dot_nt(v, g)
            sc[pl.ds(off, TILE), :] = w
            dp[pl.ds(off, TILE), :] = d
            high = w.astype(BF16)
            low = (w - high.astype(F32)).astype(BF16)
            vt = kvt[DH:, pl.ds(off, TILE)]
            return (
                total + jnp.sum(w, axis=0, keepdims=True),
                dsum + jnp.sum(w * d, axis=0, keepdims=True),
                mixed + dot_nn(vt, high) + dot_nn(vt, low),
            )

        zero = jnp.zeros((1, ROWS), F32)
        total, dsum, mixed = lax.fori_loop(0, tiles, pass_b, (zero, zero, jnp.zeros((DH, ROWS), F32)))
        inv = 1.0 / total
        delta = dsum * inv
        inv_live = inv * valid

        def pass_c(t, gq):
            off = pl.multiple_of(t * TILE, TILE)
            here = pl.ds(pl.multiple_of(off + BLOCK, BLOCK), TILE)
            p = sc[pl.ds(off, TILE), :] * inv_live
            ds = (p * (dp[pl.ds(off, TILE), :] - delta)).astype(BF16)
            dkv[here, :DH] += dot_nn(ds, q) * SCALE
            dkv[here, DH:] += dot_nn(p.astype(BF16), g)
            return gq + dot_nn(kvt[:DH, pl.ds(off, TILE)], ds)

        gq = lax.fori_loop(0, tiles, pass_c, jnp.zeros((DH, ROWS), F32))
        att = (mixed * inv_live).T.astype(BF16)
        gqr = (gq * SCALE).T.astype(BF16)
        rows = pl.ds(pl.multiple_of(base, CHUNK), CHUNK)
        for h in range(REP):
            attg[rows, h * DH : (h + 1) * DH] = att[h * CHUNK : (h + 1) * CHUNK]
            attg[rows, wide + h * DH : wide + (h + 1) * DH] = gqr[h * CHUNK : (h + 1) * CHUNK]
        return carry

    lax.fori_loop(0, (count + CHUNK - 1) // CHUNK, chunk, 0)

    slots = attg.shape[0]

    def block(b, carry):
        base = pl.multiple_of(first + b * BLOCK, BLOCK)
        win = pl.ds(base, 3 * BLOCK)
        mine = pl.ds(pl.multiple_of(b * BLOCK, BLOCK), BLOCK)
        kn = kvp[win, :DH]
        vn = kvp[win, DH:]
        kf = kg[:, :DH]
        vf = kg[:, DH:]
        q = jnp.concatenate([qg[mine, h * DH : (h + 1) * DH] for h in range(REP)], axis=0)
        g = jnp.concatenate([qg[mine, wide + h * DH : wide + (h + 1) * DH] for h in range(REP)], axis=0)
        key_tok = base - BLOCK + iota((3 * BLOCK, 1), 0)
        key_glob = jnp.sum((key_tok == pos_row).astype(F32), axis=1, keepdims=True)
        usable = (key_tok >= 0) & (key_tok < seq) & (key_glob < 0.5)
        row_tok = base + lax.rem(iota((1, ROWS), 1), BLOCK)
        live = 1.0 - jnp.sum((pos_col == row_tok).astype(F32), axis=0, keepdims=True)

        sn = jnp.where(usable, dot_nt(kn, q), NEG)
        sf = dot_nt(kf, q)
        top = jnp.maximum(jnp.max(sn, axis=0, keepdims=True), jnp.max(sf, axis=0, keepdims=True))
        wn = jnp.exp2((sn - top) * EXP2)
        wf = jnp.exp2((sf - top) * EXP2)
        dn = dot_nt(vn, g)
        df = dot_nt(vf, g)
        total = jnp.sum(wn, axis=0, keepdims=True) + jnp.sum(wf, axis=0, keepdims=True)
        dsum = jnp.sum(wn * dn, axis=0, keepdims=True) + jnp.sum(wf * df, axis=0, keepdims=True)
        inv = 1.0 / total
        delta = dsum * inv
        knt = kn.T
        vnt = vn.T
        mixed = (dot_nn(vnt, wn.astype(BF16)) + dot_nn(kgt[DH:, :], wf.astype(BF16))) * inv
        inv_live = inv * live
        pn = wn * inv_live
        pf = wf * inv_live
        dsn = (pn * (dn - delta)).astype(BF16)
        dsf = (pf * (df - delta)).astype(BF16)
        gq = (dot_nn(knt, dsn) + dot_nn(kgt[:DH, :], dsf)) * SCALE
        dkv[win, :DH] += dot_nn(dsn, q) * SCALE
        dkv[win, DH:] += dot_nn(pn.astype(BF16), g)
        dkg[:, :DH] += dot_nn(dsf, q) * SCALE
        dkg[:, DH:] += dot_nn(pf.astype(BF16), g)

        tok_col = base + iota((BLOCK, 1), 0)
        is_col = jnp.sum((tok_col == pos_row).astype(F32), axis=1, keepdims=True) > 0.5
        rank = jnp.sum((pos_row < tok_col).astype(F32), axis=1, keepdims=True).astype(jnp.int32)
        hot = (jnp.where(is_col, rank - before, -1) == iota((BLOCK, slots), 1)).astype(F32).astype(BF16)
        placed = dot_nn(hot, attg[...])
        att = mixed.T
        gqr = gq.T
        for h in range(REP):
            lo, hi = h * DH, (h + 1) * DH
            rows = slice(h * BLOCK, (h + 1) * BLOCK)
            out[mine, lo:hi] = jnp.where(is_col, placed[:, lo:hi], att[rows]).astype(BF16)
            out[mine, wide + lo : wide + hi] = jnp.where(
                is_col, placed[:, wide + lo : wide + hi], gqr[rows]
            ).astype(BF16)
        return carry

    lax.fori_loop(0, ctoks // BLOCK, block, 0)

    out_copies = []
    for step in range(GROUP):
        dst = lax.rem(z + step, GROUP)
        copy = pltpu.make_async_copy(
            out.at[pl.ds(pl.multiple_of(dst * toks, toks), toks)], qg_out[step], out_sem.at[step]
        )
        copy.start()
        out_copies.append(copy)

    far = dkg[...]
    far_high = far.astype(BF16)
    far_low = (far - far_high.astype(F32)).astype(BF16)

    def finish(t, carry):
        off = pl.multiple_of(t * TILE, TILE)
        hot = (off + iota((TILE, glob), 0) == pos_row).astype(F32).astype(BF16)
        whole = dkv[pl.ds(pl.multiple_of(off + BLOCK, BLOCK), TILE), :] + dot_nn(hot, far_high) + dot_nn(hot, far_low)
        dkv_bf[pl.ds(off, TILE), :] = whole.astype(BF16)
        return carry

    lax.fori_loop(0, tiles, finish, 0)
    last = pltpu.make_async_copy(dkv_bf, dkv_out, dkv_sem)
    last.start()
    last.wait()
    for copy in out_copies:
        copy.wait()


def post_kernel(clusters, dkv_ref, o0, o1, o2, o3, att_ref, gq_ref, dk_ref, dv_ref):
    z = lax.rem(lax.axis_index("ctx"), GROUP)
    wide = REP * DH
    for step, o in enumerate((o0, o1, o2, o3)):
        col = pl.multiple_of(lax.rem(z + GROUP - step, GROUP) * wide, wide)
        att_ref[:, pl.ds(col, wide)] = o[:, :wide]
        gq_ref[:, pl.ds(col, wide)] = o[:, wide:]
    for j in range(HK):
        whole = dkv_ref[j].astype(F32)
        for s in range(1, clusters):
            whole = whole + dkv_ref[s * GROUP + j].astype(F32)
        dk_ref[:, j * DH : (j + 1) * DH] = whole[:, :DH].astype(BF16)
        dv_ref[:, j * DH : (j + 1) * DH] = whole[:, DH:].astype(BF16)


def local(queries, keys, values, grad_out, positions):
    toks, width = queries.shape
    kwidth = keys.shape[1]
    count = lax.axis_size("ctx")
    clusters = count // GROUP
    seq = toks * count
    glob = positions.shape[0]
    vmem = pl.BlockSpec(memory_space=pltpu.VMEM)
    smem = pl.BlockSpec(memory_space=pltpu.SMEM)
    anym = pl.BlockSpec(memory_space=pl.ANY)
    params = pltpu.CompilerParams(vmem_limit_bytes=60 * 1024 * 1024)
    part = jax.ShapeDtypeStruct((toks, 2 * REP * DH), BF16)

    kv_send, *qg_send = pl.pallas_call(
        functools.partial(prep_kernel, clusters),
        out_shape=(jax.ShapeDtypeStruct((count, toks, 2 * DH), BF16),) + (part,) * GROUP,
        in_specs=[vmem] * 4,
        out_specs=(vmem,) * (GROUP + 1),
        name="prep",
    )(queries, keys, values, grad_out)

    def shift(array, step):
        pairs = [(c, c // GROUP * GROUP + (c + step) % GROUP) for c in range(count)]
        return lax.ppermute(array, "ctx", pairs)

    qg_here = [qg_send[0]] + [shift(qg_send[step], step) for step in range(1, GROUP)]
    kv_all = lax.all_to_all(kv_send, "ctx", 0, 0, tiled=True).reshape(seq, 2 * DH)
    first = lax.axis_index("ctx") // GROUP * (GROUP * toks)
    edges = first + jnp.arange(2, dtype=jnp.int32) * (GROUP * toks)
    bounds = jnp.sum((positions[None, :] < edges[:, None]).astype(jnp.int32), axis=1)

    pad = seq + 2 * BLOCK
    ctoks = GROUP * toks
    slots = 2 * CHUNK
    dkv, *outs = pl.pallas_call(
        functools.partial(main_kernel, seq, toks, glob),
        out_shape=(jax.ShapeDtypeStruct((seq, 2 * DH), BF16),) + (part,) * GROUP,
        in_specs=[smem, vmem, anym] + [anym] * GROUP,
        out_specs=(anym,) * (GROUP + 1),
        scratch_shapes=[
            pltpu.VMEM((pad, 2 * DH), BF16),
            pltpu.VMEM((2 * DH, seq), BF16),
            pltpu.VMEM((pad, 2 * DH), F32),
            pltpu.VMEM((seq, 2 * DH), BF16),
            pltpu.VMEM((ctoks, 2 * REP * DH), BF16),
            pltpu.VMEM((ctoks, 2 * REP * DH), BF16),
            pltpu.VMEM((seq, ROWS), F32),
            pltpu.VMEM((seq, ROWS), F32),
            pltpu.VMEM((slots, 2 * REP * DH), BF16),
            pltpu.VMEM((glob, 2 * DH), BF16),
            pltpu.VMEM((2 * DH, glob), BF16),
            pltpu.VMEM((glob, 2 * DH), F32),
            pltpu.SemaphoreType.DMA,
            pltpu.SemaphoreType.DMA((GROUP,)),
            pltpu.SemaphoreType.DMA((GROUP,)),
            pltpu.SemaphoreType.DMA,
        ],
        compiler_params=params,
        name="attend",
    )(bounds, positions.reshape(1, glob), kv_all, *qg_here)

    out_here = [outs[0]] + [shift(outs[step], step) for step in range(1, GROUP)]
    back = lax.all_to_all(dkv.reshape(count, toks, 2 * DH), "ctx", 0, 0, tiled=True)
    return pl.pallas_call(
        functools.partial(post_kernel, clusters),
        out_shape=(
            jax.ShapeDtypeStruct((toks, width), BF16),
            jax.ShapeDtypeStruct((toks, width), BF16),
            jax.ShapeDtypeStruct((toks, kwidth), BF16),
            jax.ShapeDtypeStruct((toks, kwidth), BF16),
        ),
        in_specs=[vmem] * (GROUP + 1),
        out_specs=(vmem,) * 4,
        name="post",
    )(back, *out_here)


def solution(mesh):
    rows = P(("dp", "ctx"), None)
    return jax.shard_map(
        local,
        mesh=mesh,
        in_specs=(rows, rows, rows, rows, P("dp")),
        out_specs=(rows, rows, rows, rows),
        check_vma=False,
    )
```

time: 1280 us -> 125 us (0.10); the launches traced: 1260 us -> 123 us
  waiting for transfers between devices: 826 us -> 63 us
  blocking collectives: 175 us -> 0 us
  other arithmetic: 140 us -> 0.7 us
  local copies, waits for them, and re-layouts: 70.2 us -> 2.86 us
  Pallas kernels: 0 us -> 28.6 us
  matrix products: 27.7 us -> 0 us
  starting transfers between devices: 7.77 us -> 27.4 us
  between operations: 14.7 us -> 0.72 us
    all_gather x2 -> x0, waiting for transfers between devices: 678 us -> none  [the longest x1 507 us: combined_all(): gathered = jax.tree.map(lambda a: lax.all_gather(a, axis), part)]
    all_gather x2 -> x0, blocking collectives: 175 us -> none  [combined_all(): gathered = jax.tree.map(lambda a: lax.all_gather(a, axis), part)]
    reduce_scatter x1 -> x0, waiting for transfers between devices: 140 us -> none  [local(): returned = lax.psum_scatter(laid, 'ctx', scatter_dimension=0, tiled=True)]
    add x66 -> x1, other arithmetic: 109 us -> 0.01 us  [local(): edges = first + jnp.arange(2, dtype=jnp.int32) * (GROUP * toks)]
    ppermute x4 -> x6, waiting for transfers between devices: 7.27 us -> 63 us  [shift(): return lax.ppermute(array, 'ctx', pairs)]
    pallas_call x0 -> x3, Pallas kernels: none -> 28.6 us  [the longest x1 22.6 us: local(): pl.pallas_call(functools.partial(main_kernel, seq, toks, glob), out_shape...]
    dot_general x18 -> x0, matrix products: 27.7 us -> none  [the longest x1 3.23 us: local(): jnp.einsum('argu,uad->argd', weight_here, value_here.astype(jnp.float32),...]
    reshape x13 -> x0, local copies, waits for them, and re-layouts: 18.1 us -> none  [the longest x1 2.89 us: local(): glob_query_grad.reshape(glob_count, query_width)]
  transfers between devices with their start and end apart: 7 -> 8, of which waited for: 6 -> 5; matrix products, arithmetic and copies ran while one was open for 6% -> 1% of each run, Pallas kernels for 0% -> 0%
where the time goes in v1:
time: 125 us; the launch traced here: 123 us
  waiting for transfers between devices  63 us (50%)
  Pallas kernels  28.6 us (23%)
  starting transfers between devices  27.4 us (22%)
  local copies, waits for them, and re-layouts  2.86 us (2%)
    ppermute x6, waiting for transfers between devices, shift(): return lax.ppermute(array, 'ctx', pairs)  63 us
    pallas_call x1, Pallas kernels, local(): pl.pallas_call(functools.partial(main_kernel, seq, toks, glob), out_shape...  22.6 us
    ppermute x6, starting transfers between devices, shift(): return lax.ppermute(array, 'ctx', pairs)  12 us
    all_to_all x1, starting transfers between devices, local(): lax.all_to_all(kv_send, 'ctx', 0, 0, tiled=True).reshape(seq, 2 * DH)  9.43 us
    all_to_all x1, starting transfers between devices, local(): lax.all_to_all(dkv.reshape(count, toks, 2 * DH), 'ctx', 0, 0, tiled=True)  5.96 us
    pallas_call x1, Pallas kernels, local(): pl.pallas_call(functools.partial(prep_kernel, clusters), out_shape=(jax.S...  3.07 us
    pallas_call x1, Pallas kernels, local(): pl.pallas_call(functools.partial(post_kernel, clusters), out_shape=(jax.S...  2.94 us
    unnamed x26, local copies, waits for them, and re-layouts  2.86 us
  transfers between devices with their start and end apart: 8, of which 5 were waited for; matrix products, arithmetic and copies ran while one was open for 1% of the time, Pallas kernels for 0%

profile of v1, /device:TPU:0, one launch (start us, length us, event | category | flops | bytes accessed | tf_op | source)
XLA Modules:
  0.0 123.3 jit_solution(2021070116047185361)
XLA Ops:
  0.6 3.1 %prep.1 = (bf16[32,128,256]{2,1,0:T(8,128)(2,1)}, bf16[128,1024]{1,0:T(8,128)(2,1)}, bf16[128,1024]{1,0:T(8,128)(2,1)}, bf16[128,1024]{1,0:T(8,128)(2,1)}, bf16[128,1024]{1,0:T(8,128)(2,1)}) custom-call(bf16[128,2048]{1,0:T(8,128)(2,1)} %q_ref.1, bf16[128,512]{1,0:T(8,128)(2,1)} %k_ref.1, bf16[128,512]{1,0:T(8,128)(2,1)} %v_ref.1, bf16[128,2048]{1,0:T(8,128)(2,1)} %g_ref.1), custom_call_target="tpu_custom_call" | custom-call | tf_op jit(solution)/shard_map/prep/pallas_call | solution.py:296
  3.7 9.4 %all-to-all-start = ((bf16[32,128,256]{2,1,0:T(8,128)(2,1)}), bf16[32,128,256]{2,1,0:T(8,128)(2,1)S(1)}, u32[]{:S(2)}, u32[]{:S(2)}) async-start(bf16[32,128,256]{2,1,0:T(8,128)(2,1)} %get-tuple-element.14), calls=%async_computation | async-start | bytes 4194304 | tf_op jit(solution)/shard_map/all_to_all | solution.py:309
  13.2 1.9 %collective-permute-start = (bf16[128,1024]{1,0:T(8,128)(2,1)}, bf16[128,1024]{1,0:T(8,128)(2,1)S(1)}, u32[]{:S(2)}, u32[]{:S(2)}) collective-permute-start(bf16[128,1024]{1,0:T(8,128)(2,1)} %get-tuple-element.16), channel_id=1, source_target_pairs={{0,1},{1,2},{2,3},{3,0},{4,5},{5,6},{6,7},{7,4},{8,9},{9,10},{10,1... | collective-permute-start | bytes 786440 | tf_op jit(solution)/shard_map/ppermute | solution.py:306
  15.0 2.7 %collective-permute-start.1 = (bf16[128,1024]{1,0:T(8,128)(2,1)S(1)}, bf16[128,1024]{1,0:T(8,128)(2,1)S(1)}, u32[]{:S(2)}, u32[]{:S(2)}) collective-permute-start(bf16[128,1024]{1,0:T(8,128)(2,1)S(1)} %copy-done.10), channel_id=1, source_target_pairs={{0,2},{1,3},{2,0},{3,1},{4,6},{5,7},{6,4},{7,5},{8,10},{9,11},{10,... | collective-permute-start | bytes 786440 | tf_op jit(solution)/shard_map/ppermute | solution.py:306
  17.7 1.5 %collective-permute-start.2 = (bf16[128,1024]{1,0:T(8,128)(2,1)S(1)}, bf16[128,1024]{1,0:T(8,128)(2,1)S(1)}, u32[]{:S(2)}, u32[]{:S(2)}) collective-permute-start(bf16[128,1024]{1,0:T(8,128)(2,1)S(1)} %copy-done.9), channel_id=1, source_target_pairs={{0,3},{1,0},{2,1},{3,2},{4,7},{5,4},{6,5},{7,6},{8,11},{9,8},{10,9... | collective-permute-start | bytes 786440 | tf_op jit(solution)/shard_map/ppermute | solution.py:306
  19.2 0.7 fusion.bounds_ref
  19.9 24.8 %collective-permute-done.refs_1_ = bf16[128,1024]{1,0:T(8,128)(2,1)S(1)} collective-permute-done((bf16[128,1024]{1,0:T(8,128)(2,1)}, bf16[128,1024]{1,0:T(8,128)(2,1)S(1)}, u32[]{:S(2)}, u32[]{:S(2)}) %collective-permute-start) | collective-permute-done | bytes 262176 | tf_op jit(solution)/shard_map/ppermute | solution.py:306
  44.6 6.3 %collective-permute-done.1.refs_2_ = bf16[128,1024]{1,0:T(8,128)(2,1)S(1)} collective-permute-done((bf16[128,1024]{1,0:T(8,128)(2,1)S(1)}, bf16[128,1024]{1,0:T(8,128)(2,1)S(1)}, u32[]{:S(2)}, u32[]{:S(2)}) %collective-permute-start.1) | collective-permute-done | bytes 262176 | tf_op jit(solution)/shard_map/ppermute | solution.py:306
  50.9 0.0 all-to-all-done
  50.9 0.7 copy-done.3
  51.6 0.1 copy-done.4
  51.7 0.7 copy-done
  52.4 22.6 %attend.1 = (bf16[4096,256]{1,0:T(8,128)(2,1)}, bf16[128,1024]{1,0:T(8,128)(2,1)}, bf16[128,1024]{1,0:T(8,128)(2,1)}, bf16[128,1024]{1,0:T(8,128)(2,1)}, bf16[128,1024]{1,0:T(8,128)(2,1)}) custom-call(s32[2]{0:T(128)} %fusion.bounds_ref, s32[1,256]{1,0:T(1,128)} %bitcast.5, bf16[4096,256]{1,0:T(8,128)(2,1)} %bitcast.3, ...), custom_call_target="tpu_custom_call" | custom-call | tf_op jit(solution)/shard_map/attend/pallas_call | solution.py:317
  75.0 6.0 %all-to-all-start.1 = ((bf16[32,128,256]{2,1,0:T(8,128)(2,1)}), bf16[32,128,256]{2,1,0:T(8,128)(2,1)S(1)}, u32[]{:S(2)}, u32[]{:S(2)}) async-start(bf16[32,128,256]{2,1,0:T(8,128)(2,1)} %bitcast.4), calls=%async_computation.1 | async-start | bytes 4194304 | tf_op jit(solution)/shard_map/all_to_all | solution.py:345
  81.0 1.9 %collective-permute-start.3 = (bf16[128,1024]{1,0:T(8,128)(2,1)}, bf16[128,1024]{1,0:T(8,128)(2,1)S(1)}, u32[]{:S(2)}, u32[]{:S(2)}) collective-permute-start(bf16[128,1024]{1,0:T(8,128)(2,1)} %get-tuple-element.21), channel_id=1, source_target_pairs={{0,1},{1,2},{2,3},{3,0},{4,5},{5,6},{6,7},{7,4},{8,9},{9,10},{10,1... | collective-permute-start | bytes 786440 | tf_op jit(solution)/shard_map/ppermute | solution.py:306
  82.8 2.7 %collective-permute-start.4 = (bf16[128,1024]{1,0:T(8,128)(2,1)S(1)}, bf16[128,1024]{1,0:T(8,128)(2,1)S(1)}, u32[]{:S(2)}, u32[]{:S(2)}) collective-permute-start(bf16[128,1024]{1,0:T(8,128)(2,1)S(1)} %copy-done.12), channel_id=1, source_target_pairs={{0,2},{1,3},{2,0},{3,1},{4,6},{5,7},{6,4},{7,5},{8,10},{9,11},{10,... | collective-permute-start | bytes 786440 | tf_op jit(solution)/shard_map/ppermute | solution.py:306
  85.5 1.5 %collective-permute-start.5 = (bf16[128,1024]{1,0:T(8,128)(2,1)S(1)}, bf16[128,1024]{1,0:T(8,128)(2,1)S(1)}, u32[]{:S(2)}, u32[]{:S(2)}) collective-permute-start(bf16[128,1024]{1,0:T(8,128)(2,1)S(1)} %copy-done.11), channel_id=1, source_target_pairs={{0,3},{1,0},{2,1},{3,2},{4,7},{5,4},{6,5},{7,6},{8,11},{9,8},{10,9... | collective-permute-start | bytes 786440 | tf_op jit(solution)/shard_map/ppermute | solution.py:306
  87.0 24.4 %collective-permute-done.3.o1 = bf16[128,1024]{1,0:T(8,128)(2,1)S(1)} collective-permute-done((bf16[128,1024]{1,0:T(8,128)(2,1)}, bf16[128,1024]{1,0:T(8,128)(2,1)S(1)}, u32[]{:S(2)}, u32[]{:S(2)}) %collective-permute-start.3) | collective-permute-done | bytes 262176 | tf_op jit(solution)/shard_map/ppermute | solution.py:306
  111.4 6.1 %collective-permute-done.4.o2 = bf16[128,1024]{1,0:T(8,128)(2,1)S(1)} collective-permute-done((bf16[128,1024]{1,0:T(8,128)(2,1)S(1)}, bf16[128,1024]{1,0:T(8,128)(2,1)S(1)}, u32[]{:S(2)}, u32[]{:S(2)}) %collective-permute-start.4) | collective-permute-done | bytes 262176 | tf_op jit(solution)/shard_map/ppermute | solution.py:306
  117.5 1.5 %collective-permute-done.5.o3 = bf16[128,1024]{1,0:T(8,128)(2,1)S(1)} collective-permute-done((bf16[128,1024]{1,0:T(8,128)(2,1)S(1)}, bf16[128,1024]{1,0:T(8,128)(2,1)S(1)}, u32[]{:S(2)}, u32[]{:S(2)}) %collective-permute-start.5) | collective-permute-done | bytes 262176 | tf_op jit(solution)/shard_map/ppermute | solution.py:306
  119.0 0.0 all-to-all-done.1.dkv_ref
  119.0 0.7 copy-done.7
  119.7 0.7 copy-done.1
  120.4 2.9 %post.1 = (bf16[128,2048]{1,0:T(8,128)(2,1)}, bf16[128,2048]{1,0:T(8,128)(2,1)}, bf16[128,512]{1,0:T(8,128)(2,1)}, bf16[128,512]{1,0:T(8,128)(2,1)}) custom-call(bf16[32,128,256]{2,1,0:T(8,128)(2,1)} %copy-done.1, bf16[128,1024]{1,0:T(8,128)(2,1)} %get-tuple-element.20.o0, bf16[128,1024]{1,0:T(8,128)(2,1)} %copy-done.5, bf16[128,1024]{1,0:T(8,128)(2,1)} %copy-done.6, ...), custom_call_target="tpu_custom_call" | custom-call | tf_op jit(solution)/shard_map/post/pallas_call | solution.py:346
  (23 shorter events, 0.0 us)
Async XLA Ops:
  3.7 11.3 %copy-start.10 = (bf16[128,1024]{1,0:T(8,128)(2,1)S(1)}, bf16[128,1024]{1,0:T(8,128)(2,1)}, u32[]{:S(2)}) copy-start(bf16[128,1024]{1,0:T(8,128)(2,1)} %get-tuple-element.17) | copy-start | bytes 786436
  3.7 14.0 %copy-start.9 = (bf16[128,1024]{1,0:T(8,128)(2,1)S(1)}, bf16[128,1024]{1,0:T(8,128)(2,1)}, u32[]{:S(2)}) copy-start(bf16[128,1024]{1,0:T(8,128)(2,1)} %get-tuple-element.18) | copy-start | bytes 786436
  3.7 15.5 %copy-start.8 = (s32[256]{0:T(256)S(1)}, s32[256]{0:T(256)}, u32[]{:S(2)}) copy-start(s32[256]{0:T(256)} %param.9) | copy-start | bytes 3076
  3.7 47.2 %all-to-all-start = ((bf16[32,128,256]{2,1,0:T(8,128)(2,1)}), bf16[32,128,256]{2,1,0:T(8,128)(2,1)S(1)}, u32[]{:S(2)}, u32[]{:S(2)}) async-start(bf16[32,128,256]{2,1,0:T(8,128)(2,1)} %get-tuple-element.14), calls=%async_computation | async-start | bytes 4194304 | tf_op jit(solution)/shard_map/all_to_all | solution.py:309
  13.2 31.5 %collective-permute-start = (bf16[128,1024]{1,0:T(8,128)(2,1)}, bf16[128,1024]{1,0:T(8,128)(2,1)S(1)}, u32[]{:S(2)}, u32[]{:S(2)}) collective-permute-start(bf16[128,1024]{1,0:T(8,128)(2,1)} %get-tuple-element.16), channel_id=1, source_target_pairs={{0,1},{1,2},{2,3},{3,0},{4,5},{5,6},{6,7},{7,4},{8,9},{9,10},{10,1... | collective-permute-start | bytes 786440 | tf_op jit(solution)/shard_map/ppermute | solution.py:306
  15.0 35.9 %collective-permute-start.1 = (bf16[128,1024]{1,0:T(8,128)(2,1)S(1)}, bf16[128,1024]{1,0:T(8,128)(2,1)S(1)}, u32[]{:S(2)}, u32[]{:S(2)}) collective-permute-start(bf16[128,1024]{1,0:T(8,128)(2,1)S(1)} %copy-done.10), channel_id=1, source_target_pairs={{0,2},{1,3},{2,0},{3,1},{4,6},{5,7},{6,4},{7,5},{8,10},{9,11},{10,... | collective-permute-start | bytes 786440 | tf_op jit(solution)/shard_map/ppermute | solution.py:306
  17.7 33.2 %collective-permute-start.2 = (bf16[128,1024]{1,0:T(8,128)(2,1)S(1)}, bf16[128,1024]{1,0:T(8,128)(2,1)S(1)}, u32[]{:S(2)}, u32[]{:S(2)}) collective-permute-start(bf16[128,1024]{1,0:T(8,128)(2,1)S(1)} %copy-done.9), channel_id=1, source_target_pairs={{0,3},{1,0},{2,1},{3,2},{4,7},{5,4},{6,5},{7,6},{8,11},{9,8},{10,9... | collective-permute-start | bytes 786440 | tf_op jit(solution)/shard_map/ppermute | solution.py:306
  44.6 6.3 %copy-start.2 = (bf16[128,1024]{1,0:T(8,128)(2,1)}, bf16[128,1024]{1,0:T(8,128)(2,1)S(1)}, u32[]{:S(2)}) copy-start(bf16[128,1024]{1,0:T(8,128)(2,1)S(1)} %collective-permute-done.refs_1_) | copy-start | bytes 786436
  50.9 0.7 copy-start.3
  50.9 0.8 copy-start.4
  50.9 1.5 %copy-start = (bf16[32,128,256]{2,1,0:T(8,128)(2,1)}, bf16[32,128,256]{2,1,0:T(8,128)(2,1)S(1)}, u32[]{:S(2)}) copy-start(bf16[32,128,256]{2,1,0:T(8,128)(2,1)S(1)} %all-to-all-done) | copy-start | bytes 6291460
  75.0 7.8 %copy-start.12 = (bf16[128,1024]{1,0:T(8,128)(2,1)S(1)}, bf16[128,1024]{1,0:T(8,128)(2,1)}, u32[]{:S(2)}) copy-start(bf16[128,1024]{1,0:T(8,128)(2,1)} %get-tuple-element.22) | copy-start | bytes 786436
  75.0 10.5 %copy-start.11 = (bf16[128,1024]{1,0:T(8,128)(2,1)S(1)}, bf16[128,1024]{1,0:T(8,128)(2,1)}, u32[]{:S(2)}) copy-start(bf16[128,1024]{1,0:T(8,128)(2,1)} %get-tuple-element.23) | copy-start | bytes 786436
  75.0 44.0 %all-to-all-start.1 = ((bf16[32,128,256]{2,1,0:T(8,128)(2,1)}), bf16[32,128,256]{2,1,0:T(8,128)(2,1)S(1)}, u32[]{:S(2)}, u32[]{:S(2)}) async-start(bf16[32,128,256]{2,1,0:T(8,128)(2,1)} %bitcast.4), calls=%async_computation.1 | async-start | bytes 4194304 | tf_op jit(solution)/shard_map/all_to_all | solution.py:345
  81.0 30.4 %collective-permute-start.3 = (bf16[128,1024]{1,0:T(8,128)(2,1)}, bf16[128,1024]{1,0:T(8,128)(2,1)S(1)}, u32[]{:S(2)}, u32[]{:S(2)}) collective-permute-start(bf16[128,1024]{1,0:T(8,128)(2,1)} %get-tuple-element.21), channel_id=1, source_target_pairs={{0,1},{1,2},{2,3},{3,0},{4,5},{5,6},{6,7},{7,4},{8,9},{9,10},{10,1... | collective-permute-start | bytes 786440 | tf_op jit(solution)/shard_map/ppermute | solution.py:306
  82.8 34.7 %collective-permute-start.4 = (bf16[128,1024]{1,0:T(8,128)(2,1)S(1)}, bf16[128,1024]{1,0:T(8,128)(2,1)S(1)}, u32[]{:S(2)}, u32[]{:S(2)}) collective-permute-start(bf16[128,1024]{1,0:T(8,128)(2,1)S(1)} %copy-done.12), channel_id=1, source_target_pairs={{0,2},{1,3},{2,0},{3,1},{4,6},{5,7},{6,4},{7,5},{8,10},{9,11},{10,... | collective-permute-start | bytes 786440 | tf_op jit(solution)/shard_map/ppermute | solution.py:306
  85.5 33.5 %collective-permute-start.5 = (bf16[128,1024]{1,0:T(8,128)(2,1)S(1)}, bf16[128,1024]{1,0:T(8,128)(2,1)S(1)}, u32[]{:S(2)}, u32[]{:S(2)}) collective-permute-start(bf16[128,1024]{1,0:T(8,128)(2,1)S(1)} %copy-done.11), channel_id=1, source_target_pairs={{0,3},{1,0},{2,1},{3,2},{4,7},{5,4},{6,5},{7,6},{8,11},{9,8},{10,9... | collective-permute-start | bytes 786440 | tf_op jit(solution)/shard_map/ppermute | solution.py:306
  111.4 7.6 %copy-start.5 = (bf16[128,1024]{1,0:T(8,128)(2,1)}, bf16[128,1024]{1,0:T(8,128)(2,1)S(1)}, u32[]{:S(2)}) copy-start(bf16[128,1024]{1,0:T(8,128)(2,1)S(1)} %collective-permute-done.3.o1) | copy-start | bytes 786436
  117.5 1.5 %copy-start.6 = (bf16[128,1024]{1,0:T(8,128)(2,1)}, bf16[128,1024]{1,0:T(8,128)(2,1)S(1)}, u32[]{:S(2)}) copy-start(bf16[128,1024]{1,0:T(8,128)(2,1)S(1)} %collective-permute-done.4.o2) | copy-start | bytes 786436
  118.9 0.7 copy-start.7
  119.0 1.4 %copy-start.1 = (bf16[32,128,256]{2,1,0:T(8,128)(2,1)}, bf16[32,128,256]{2,1,0:T(8,128)(2,1)S(1)}, u32[]{:S(2)}) copy-start(bf16[32,128,256]{2,1,0:T(8,128)(2,1)S(1)} %all-to-all-done.1.dkv_ref) | copy-start | bytes 6291460
